TPU v7x, 256 devices: a whole 4x4x8 slice. The times are simulated.
256 devices in a mesh: row: 16 (over z_lo, x, core), col: 16 (over z_hi, y).
Axes of the slice: x: 4, y: 4, z: 8 (z_hi: 4, z_lo: 2; z = z_hi * 2 + z_lo), core: 2. Of those that a mesh axis runs over, the one named last changes fastest.
Arguments:
- blocks_inverse: bfloat16 [12288, 12288], P('row', 'col'), as said below
- factor_rows: bfloat16 [2, 6144, 256], P(None, 'row'), may hold values from -0.15234375 to 0.15234375
- block_lists: int32 [2, 48], replicated, may hold values from 0 to 95, as said below
- diag_inverse: float32 [2, 256, 256], replicated, as said below
Outputs:
- column_inverse: float32 [2, 12288, 256], P(None, 'row')
- mirror_inverse: float32 [2, 256, 12288], P(None, None, 'col')
- diagonal_inverse: float32 [2, 256, 256], replicated
Inputs may be any that keep to these rules, and one draw needn't show every extreme that they name: blocks_inverse is exactly symmetric and positive definite. block_lists[s, m] is 2 * m or 2 * m + 1. diag_inverse[s] is symmetric.
All inputs are finite; a program needn't handle non-finite values.
Results may differ from a plain program's by a relative error of at most 0.0003.
Values may be sent and summed in bfloat16 or wider, within the bound.
A program may use at most 64 MiB of HBM per device.

v0:
```python
import jax
import jax.numpy as jnp
from jax import lax
from jax.sharding import PartitionSpec as P

BS = 128


def broadcast(x, axis, root):
    mine = lax.axis_index(axis) == root
    return lax.psum(jnp.where(mine, x, jnp.zeros_like(x)), axis)


def pair_bits(block_lists, first_block, block_count):
    local_lists = lax.dynamic_slice_in_dim(block_lists, first_block // 2, block_count // 2, 1)
    pair_first = 2 * (first_block // 2 + jnp.arange(block_count // 2, dtype=jnp.int32))
    return local_lists - pair_first[None, :]


def expand_pairs(packed, bits):
    sup_count = packed.shape[0]
    feature_count = packed.shape[2]
    pairs = bits.shape[1]
    grouped = packed.reshape(sup_count, pairs, 1, BS, feature_count)
    which = (
        bits[:, :, None, None, None] == jnp.arange(2, dtype=jnp.int32)[None, None, :, None, None]
    )
    dense = jnp.where(which, grouped, jnp.zeros((), packed.dtype))
    return dense.reshape(sup_count, pairs * 2 * BS, feature_count)


def compact_pairs(dense, bits):
    sup_count = dense.shape[0]
    feature_count = dense.shape[2]
    pairs = bits.shape[1]
    grouped = dense.reshape(sup_count, pairs, 2, BS, feature_count)
    chosen = jnp.where(bits[:, :, None, None] == 0, grouped[:, :, 0], grouped[:, :, 1])
    return chosen.reshape(sup_count, pairs * BS, feature_count)


def multiply_each(matrix, stacked):
    results = []
    for sup_index in range(stacked.shape[0]):
        results.append(
            jnp.dot(matrix, stacked[sup_index].astype(jnp.float32), precision=lax.Precision.HIGHEST)
        )
    return jnp.stack(results)


def local(blocks_inverse, factor_rows, block_lists, diag_inverse):
    row_index = lax.axis_index("row")
    col_index = lax.axis_index("col")
    row_blocks = blocks_inverse.shape[0] // BS
    col_blocks = blocks_inverse.shape[1] // BS
    row_bits = pair_bits(block_lists, row_index * row_blocks, row_blocks)
    col_bits = pair_bits(block_lists, col_index * col_blocks, col_blocks)
    packed_length = col_blocks // 2 * BS
    root_row = col_index * col_blocks // row_blocks
    gathered = lax.all_gather(factor_rows, "row", axis=1, tiled=True)
    column_packed = lax.dynamic_slice_in_dim(gathered, col_index * packed_length, packed_length, 1)
    column_dense = expand_pairs(column_packed, col_bits)
    blocks_wide = blocks_inverse.astype(jnp.float32)
    products = multiply_each(blocks_wide, column_dense)
    listed_products = compact_pairs(products, row_bits)
    diagonal_terms = jnp.einsum(
        "srw,srv->swv",
        factor_rows.astype(jnp.float32),
        listed_products,
        precision=lax.Precision.HIGHEST,
    )
    diagonal_inverse = diag_inverse + lax.psum(diagonal_terms, ("row", "col"))
    row_total = lax.psum(listed_products, "col")
    column_inverse = -expand_pairs(row_total, row_bits)
    mirror_total = broadcast(row_total, "row", root_row)
    mirror_inverse = jnp.transpose(-expand_pairs(mirror_total, col_bits), (0, 2, 1))
    return (column_inverse, mirror_inverse, diagonal_inverse)


def solution(mesh):
    return jax.shard_map(
        local,
        mesh=mesh,
        in_specs=(P("row", "col"), P(None, "row", None), P(), P()),
        out_specs=(P(None, "row", None), P(None, None, "col"), P()),
        check_vma=False,
    )
```

profile of v0, /device:TPU:1, one launch (start us, length us, event | category | flops | bytes accessed | tf_op | source)
XLA Modules:
  0.0 641.8 jit_solution(4474671392308871341)
XLA Ops:
  7.2 0.0 copy-start
  7.2 0.0 all-gather.2.cloned.1.call-start
  7.2 0.7 all-gather.2.cloned.1.call-update
  8.0 0.8 broadcast_compare_fusion
  8.7 0.1 broadcast_bitcast_fusion
  8.8 0.8 dynamic-slice_subtract_fusion
  9.6 0.1 iota_compare_fusion
  9.6 49.3 %all-gather.2.cloned.1.call-done = bf16[2,6144,256]{2,1,0:T(8,128)(2,1)} async-done(((bf16[2,384,256]{2,1,0:T(8,128)(2,1)}), bf16[2,6144,256]{2,1,0:T(8,128)(2,1)}) %all-gather.2.cloned.1.call-update) | async-done | bytes 6291472 | tf_op jit(solution)/shard_map/all_gather | solution.py:59
  59.0 1.0 constant_dynamic-slice_fusion
  60.0 0.1 broadcast_select_fusion
  60.1 0.8 fusion.1
  60.9 0.5 convolution_bitcast_fusion.1
  61.4 0.4 stack.9
  61.9 1.5 convolution_bitcast_fusion
  63.4 0.4 stack.10
  63.8 0.3 constant_dynamic-update-slice_fusion.1
  64.1 0.3 constant_dynamic-update-slice_fusion
  64.4 1.2 fusion
  65.6 1.0 copy.11
  66.6 1.0 copy.10
  67.6 0.2 broadcast_select_fusion.2
  67.8 0.0 copy-start.1
  67.8 3.0 convolution_bitcast_fusion.2
  70.8 0.7 all-reduce.4.cloned.1.call-update
  71.5 0.0 copy-start.3
  71.5 0.0 all-reduce.8.cloned.1.call-start
  71.6 0.7 all-reduce.8.cloned.1.call-update
  72.2 0.0 all-reduce.6.cloned.1.call-start
  72.3 160.2 %all-reduce.4.cloned.1.call-done = f32[2,384,256]{2,1,0:T(8,128)} async-done(((f32[2,384,256]{2,1,0:T(8,128)}), f32[2,384,256]{2,1,0:T(8,128)}) %all-reduce.4.cloned.1.call-update) | async-done | bytes 786448 | tf_op jit(solution)/shard_map/psum | solution.py:72
  232.5 0.9 broadcast_select_fusion.1
  233.5 0.0 all-reduce.6.cloned.1.call-update
  233.5 0.1 iota_compare_fusion.1
  233.6 0.1 broadcast_in_dim.93
  233.7 0.1 broadcast_in_dim.107
  233.8 0.2 copy.15
  234.0 267.5 %all-reduce.8.cloned.1.call-done = f32[2,256,256]{1,2,0:T(8,128)} async-done(((f32[2,256,256]{1,2,0:T(8,128)}), f32[2,256,256]{1,2,0:T(8,128)}) %all-reduce.8.cloned.1.call-update) | async-done | bytes 524304 | tf_op jit(solution)/shard_map/psum | solution.py:71
  501.5 1.1 add.48
  502.6 1.0 copy.17
  503.6 0.4 copy.12
  504.0 1.7 broadcast_in_dim.104
  505.7 2.5 broadcast_in_dim.105
  508.2 1.3 select_negate_fusion
  509.5 3.0 copy.16
  512.5 115.7 %all-reduce.6.cloned.1.call-done = f32[2,3,128,256]{3,2,1,0:T(8,128)} async-done(((f32[2,3,128,256]{3,2,1,0:T(8,128)}), f32[2,3,128,256]{3,2,1,0:T(8,128)}) %all-reduce.6.cloned.1.call-update) | async-done | bytes 786448 | tf_op jit(solution)/shard_map/psum | solution.py:11
  628.2 1.5 copy.13
  629.8 1.7 broadcast_in_dim.112
  631.4 2.5 broadcast_in_dim.113
  634.0 1.3 negate_bitcast_fusion
  (11 shorter events, 0.1 us)
Async XLA Ops:
  7.2 53.8 %copy-start = (bf16[768,768]{1,0:T(8,128)(2,1)S(1)}, bf16[768,768]{1,0:T(8,128)(2,1)}, u32[]{:S(2)}) copy-start(bf16[768,768]{1,0:T(8,128)(2,1)} %param.4) | copy-start | bytes 3538948
  7.2 51.8 %all-gather.2.cloned.1.call-start = ((), (), s32[]{:S(2)}) async-start(), calls=%async_computation | async-start | bytes 6684672 | tf_op jit(solution)/shard_map/all_gather | solution.py:59
  67.8 3.0 copy-start.1
  70.8 161.8 %all-reduce.4.cloned.1.call-start = ((), (), s32[]{:S(2)}) async-start(), calls=%async_computation.1 | async-start | bytes 1572864 | tf_op jit(solution)/shard_map/psum | solution.py:72
  71.5 162.3 %copy-start.3 = (f32[2,256,256]{2,1,0:T(8,128)S(1)}, f32[2,256,256]{2,1,0:T(8,128)}, u32[]{:S(2)}) copy-start(f32[2,256,256]{2,1,0:T(8,128)} %param.7) | copy-start | bytes 1572868
  71.5 430.0 %all-reduce.8.cloned.1.call-start = ((), (), s32[]{:S(2)}) async-start(), calls=%async_computation.3 | async-start | bytes 1048576 | tf_op jit(solution)/shard_map/psum | solution.py:71
  72.2 556.0 %all-reduce.6.cloned.1.call-start = ((), (), s32[]{:S(2)}) async-start(), calls=%async_computation.2 | async-start | bytes 1572864 | tf_op jit(solution)/shard_map/psum | solution.py:11
  234.0 269.6 %copy-start.2 = (f32[2,384,256]{2,1,0:T(8,128)S(1)}, f32[2,384,256]{2,1,0:T(8,128)}, u32[]{:S(2)}) copy-start(f32[2,384,256]{2,1,0:T(8,128)} %all-reduce.4.cloned.1.call-done) | copy-start | bytes 2359300
Sparse Core Ops, SparseCore 0:
  9.8 49.1 all-gather.1
  74.8 157.7 all-reduce.3
  238.6 262.8 all-reduce.7
  504.0 124.2 all-reduce.5
where the time goes:
time: 642 us
  waiting for transfers between devices  595 us (93%)
  local copies, waits for them, and re-layouts  21.3 us (3%)
  between operations  14 us (2%)
  other arithmetic  6.57 us (1%)
    psum x1, waiting for transfers between devices, local(): diagonal_inverse = diag_inverse + lax.psum(diagonal_terms, ('row', 'col'))  268 us
    psum x1, waiting for transfers between devices, local(): row_total = lax.psum(listed_products, 'col')  160 us
    psum x1, waiting for transfers between devices, broadcast(): return lax.psum(jnp.where(mine, x, jnp.zeros_like(x)), axis)  116 us
    all_gather x1, waiting for transfers between devices, local(): gathered = lax.all_gather(factor_rows, 'row', axis=1, tiled=True)  49.3 us
  transfers between devices with their start and end apart: 4, of which 4 were waited for; matrix products, arithmetic and copies ran while one was open for 2% of the time, Pallas kernels for 0%

commit v1 on v0

--- a/solution.py
+++ b/solution.py
@@ -56,7 +56,16 @@
     col_bits = pair_bits(block_lists, col_index * col_blocks, col_blocks)
     packed_length = col_blocks // 2 * BS
     root_row = col_index * col_blocks // row_blocks
-    gathered = lax.all_gather(factor_rows, "row", axis=1, tiled=True)
+
+    def manage_trails_over_axis(t0):
+        return jnp.concatenate(
+            jax.lax.all_to_all(
+                jnp.stack([t0 for _ in range(jax.lax.axis_size("row"))]), "row", 0, 0
+            ),
+            axis=1,
+        )
+
+    gathered = manage_trails_over_axis(factor_rows)
     column_packed = lax.dynamic_slice_in_dim(gathered, col_index * packed_length, packed_length, 1)
     column_dense = expand_pairs(column_packed, col_bits)
     blocks_wide = blocks_inverse.astype(jnp.float32)

time: 642 us -> 706 us (1.100)
  waiting for transfers between devices: 595 us -> 640 us
  local copies, waits for them, and re-layouts: 21.3 us -> 32.9 us
  starting transfers between devices: 0.12 us -> 7.95 us
    all_to_all x0 -> x1, waiting for transfers between devices: none -> 87.3 us  [manage_trails_over_axis(): jax.lax.all_to_all(jnp.stack([t0 for _ in range(jax.lax.axis_size('row'))...]
    all_gather x1 -> x0, waiting for transfers between devices: 49.3 us -> none  [local(): gathered = lax.all_gather(factor_rows, 'row', axis=1, tiled=True)]
    psum x1, waiting for transfers between devices: 160 us -> 168 us  [local(): row_total = lax.psum(listed_products, 'col')]
    all_to_all x0 -> x1, starting transfers between devices: none -> 7.7 us  [manage_trails_over_axis(): jax.lax.all_to_all(jnp.stack([t0 for _ in range(jax.lax.axis_size('row'))...]
where the time goes in v1:
time: 706 us; the launch traced here: 705 us
  waiting for transfers between devices  640 us (91%)
  local copies, waits for them, and re-layouts  32.9 us (5%)
  between operations  14 us (2%)
  starting transfers between devices  7.95 us (1%)
    psum x1, waiting for transfers between devices, local(): diagonal_inverse = diag_inverse + lax.psum(diagonal_terms, ('row', 'col'))  268 us
    psum x1, waiting for transfers between devices, local(): row_total = lax.psum(listed_products, 'col')  168 us
    psum x1, waiting for transfers between devices, broadcast(): return lax.psum(jnp.where(mine, x, jnp.zeros_like(x)), axis)  116 us
    all_to_all x1, waiting for transfers between devices, manage_trails_over_axis(): jax.lax.all_to_all(jnp.stack([t0 for _ in range(jax.lax.axis_size('row'))...  87.3 us
  transfers between devices with their start and end apart: 4, of which 4 were waited for; matrix products, arithmetic and copies ran while one was open for 2% of the time, Pallas kernels for 0%

profile of v1, /device:TPU:1, one launch (start us, length us, event | category | flops | bytes accessed | tf_op | source)
XLA Modules:
  0.0 705.2 jit_solution(3591739759308006651)
XLA Ops:
  7.2 0.0 copy-start
  7.2 4.4 stack.8
  11.6 7.7 %all-to-all-start = ((bf16[16,2,384,256]{3,2,1,0:T(8,128)(2,1)}), bf16[16,2,384,256]{3,2,1,0:T(8,128)(2,1)}, u32[]{:S(2)}, u32[]{:S(2)}) async-start(bf16[16,2,384,256]{3,2,1,0:T(8,128)(2,1)} %stack.8), calls=%async_computation | async-start | bytes 12582912 | tf_op jit(solution)/shard_map/all_to_all | solution.py:62
  19.3 0.1 broadcast_compare_fusion
  19.4 0.1 broadcast_bitcast_fusion
  19.5 0.1 dynamic-slice_subtract_fusion
  19.6 0.1 iota_compare_fusion
  19.7 87.3 %all-to-all-done = bf16[16,2,384,256]{3,2,1,0:T(8,128)(2,1)} async-done(((bf16[16,2,384,256]{3,2,1,0:T(8,128)(2,1)}), bf16[16,2,384,256]{3,2,1,0:T(8,128)(2,1)}, u32[]{:S(2)}, u32[]{:S(2)}) %all-to-all-start) | async-done | bytes 6291488 | tf_op jit(solution)/shard_map/all_to_all | solution.py:62
  106.9 3.2 copy.26
  110.2 0.1 broadcast_select_fusion
  110.3 0.8 fusion.1
  111.1 0.5 convolution_bitcast_fusion.1
  111.6 0.4 stack.9
  112.1 0.3 constant_dynamic-update-slice_fusion.1
  112.3 0.7 copy-done.3
  113.0 1.4 convolution_bitcast_fusion
  114.4 1.5 stack.10
  116.0 0.3 constant_dynamic-update-slice_fusion
  116.3 2.1 fusion
  118.4 2.2 copy.27
  120.6 2.1 copy.28
  122.6 1.3 broadcast_select_fusion.2
  124.0 0.0 copy-start.1
  124.0 1.7 convolution_bitcast_fusion.2
  125.7 0.7 all-reduce.4.cloned.1.call-update
  126.4 0.0 all-reduce.8.cloned.1.call-start
  126.5 0.7 all-reduce.8.cloned.1.call-update
  127.2 0.2 all-reduce.6.cloned.1.call-start
  127.4 168.4 %all-reduce.4.cloned.1.call-done = f32[2,384,256]{2,1,0:T(8,128)} async-done(((f32[2,384,256]{2,1,0:T(8,128)}), f32[2,384,256]{2,1,0:T(8,128)}) %all-reduce.4.cloned.1.call-update) | async-done | bytes 786448 | tf_op jit(solution)/shard_map/psum | solution.py:81
  295.8 0.9 broadcast_select_fusion.1
  296.7 0.0 all-reduce.6.cloned.1.call-update
  296.7 0.1 iota_compare_fusion.1
  296.8 0.1 broadcast_in_dim.93
  296.9 0.1 broadcast_in_dim.107
  297.0 0.2 copy.32
  297.2 267.5 %all-reduce.8.cloned.1.call-done = f32[2,256,256]{1,2,0:T(8,128)} async-done(((f32[2,256,256]{1,2,0:T(8,128)}), f32[2,256,256]{1,2,0:T(8,128)}) %all-reduce.8.cloned.1.call-update) | async-done | bytes 524304 | tf_op jit(solution)/shard_map/psum | solution.py:80
  564.8 1.1 add.48
  565.9 1.0 copy.34
  566.9 0.4 copy.29
  567.2 1.7 broadcast_in_dim.104
  568.9 2.5 broadcast_in_dim.105
  571.5 1.3 select_negate_fusion
  572.8 3.0 copy.33
  575.8 115.9 %all-reduce.6.cloned.1.call-done = f32[2,3,128,256]{3,2,1,0:T(8,128)} async-done(((f32[2,3,128,256]{3,2,1,0:T(8,128)}), f32[2,3,128,256]{3,2,1,0:T(8,128)}) %all-reduce.6.cloned.1.call-update) | async-done | bytes 786448 | tf_op jit(solution)/shard_map/psum | solution.py:11
  691.7 1.5 copy.30
  693.2 1.7 broadcast_in_dim.112
  694.9 2.5 broadcast_in_dim.113
  697.4 1.3 negate_bitcast_fusion
  (18 shorter events, 0.1 us)
Async XLA Ops:
  7.2 103.9 %copy-start = (bf16[768,768]{1,0:T(8,128)(2,1)S(1)}, bf16[768,768]{1,0:T(8,128)(2,1)}, u32[]{:S(2)}) copy-start(bf16[768,768]{1,0:T(8,128)(2,1)} %param.4) | copy-start | bytes 3538948
  11.6 7.7 %copy-start.6 = (s32[2,48]{1,0:T(2,128)S(1)}, s32[2,48]{1,0:T(2,128)}, u32[]{:S(2)}) copy-start(s32[2,48]{1,0:T(2,128)} %param.6) | copy-start | bytes 1156
  11.6 95.3 %all-to-all-start = ((bf16[16,2,384,256]{3,2,1,0:T(8,128)(2,1)}), bf16[16,2,384,256]{3,2,1,0:T(8,128)(2,1)}, u32[]{:S(2)}, u32[]{:S(2)}) async-start(bf16[16,2,384,256]{3,2,1,0:T(8,128)(2,1)} %stack.8), calls=%async_computation | async-start | bytes 12582912 | tf_op jit(solution)/shard_map/all_to_all | solution.py:62
  112.0 1.0 copy-start.3
  122.6 1.4 copy-start.4
  124.0 1.7 copy-start.1
  125.7 170.1 %all-reduce.4.cloned.1.call-start = ((), (), s32[]{:S(2)}) async-start(), calls=%async_computation.1 | async-start | bytes 1572864 | tf_op jit(solution)/shard_map/psum | solution.py:81
  126.4 170.6 %copy-start.5 = (f32[2,256,256]{2,1,0:T(8,128)S(1)}, f32[2,256,256]{2,1,0:T(8,128)}, u32[]{:S(2)}) copy-start(f32[2,256,256]{2,1,0:T(8,128)} %param.7) | copy-start | bytes 1572868
  126.4 438.3 %all-reduce.8.cloned.1.call-start = ((), (), s32[]{:S(2)}) async-start(), calls=%async_computation.3 | async-start | bytes 1048576 | tf_op jit(solution)/shard_map/psum | solution.py:80
  127.2 564.5 %all-reduce.6.cloned.1.call-start = ((), (), s32[]{:S(2)}) async-start(), calls=%async_computation.2 | async-start | bytes 1572864 | tf_op jit(solution)/shard_map/psum | solution.py:11
  297.2 269.6 %copy-start.2 = (f32[2,384,256]{2,1,0:T(8,128)S(1)}, f32[2,384,256]{2,1,0:T(8,128)}, u32[]{:S(2)}) copy-start(f32[2,384,256]{2,1,0:T(8,128)} %all-reduce.4.cloned.1.call-done) | copy-start | bytes 2359300
Sparse Core Ops, SparseCore 0:
  129.7 166.0 all-reduce.3
  301.8 262.8 all-reduce.7
  567.4 124.2 all-reduce.5

commit v2 on v0

--- a/solution.py
+++ b/solution.py
@@ -4,6 +4,11 @@
 from jax.sharding import PartitionSpec as P
 
 BS = 128
+
+
+def check_ticks(raw, axis_key, which_axis):
+    shaped = jax.lax.psum(raw, axis_name=axis_key)
+    return jax.lax.psum(shaped, axis_name=which_axis)
 
 
 def broadcast(x, axis, root):
@@ -68,7 +73,7 @@
         listed_products,
         precision=lax.Precision.HIGHEST,
     )
-    diagonal_inverse = diag_inverse + lax.psum(diagonal_terms, ("row", "col"))
+    diagonal_inverse = diag_inverse + check_ticks(diagonal_terms, "col", "row")
     row_total = lax.psum(listed_products, "col")
     column_inverse = -expand_pairs(row_total, row_bits)
     mirror_total = broadcast(row_total, "row", root_row)

time: 642 us -> 384 us (0.60)
  waiting for transfers between devices: 595 us -> 338 us
    psum x1 -> x0, waiting for transfers between devices: 268 us -> none  [local(): diagonal_inverse = diag_inverse + lax.psum(diagonal_terms, ('row', 'col'))]
    psum x1, waiting for transfers between devices: 116 us -> 126 us  [broadcast(): return lax.psum(jnp.where(mine, x, jnp.zeros_like(x)), axis)]
  transfers between devices with their start and end apart: 4 -> 3, of which waited for: 4 -> 3; matrix products, arithmetic and copies ran while one was open for 2% -> 3% of each run, Pallas kernels for 0% -> 0%
where the time goes in v2:
time: 384 us
  waiting for transfers between devices  338 us (88%)
  local copies, waits for them, and re-layouts  21.6 us (6%)
  between operations  14 us (4%)
  other arithmetic  6.67 us (2%)
    psum x1, waiting for transfers between devices, local(): row_total = lax.psum(listed_products, 'col')  162 us
    psum x1, waiting for transfers between devices, broadcast(): return lax.psum(jnp.where(mine, x, jnp.zeros_like(x)), axis)  126 us
    all_gather x1, waiting for transfers between devices, local(): gathered = lax.all_gather(factor_rows, 'row', axis=1, tiled=True)  49.3 us
    broadcast_in_dim x9, local copies, waits for them, and re-layouts, expand_pairs(): dense = jnp.where(which, grouped, jnp.zeros((), packed.dtype))  9.01 us
  transfers between devices with their start and end apart: 3, of which 3 were waited for; matrix products, arithmetic and copies ran while one was open for 3% of the time, Pallas kernels for 0%

profile of v2, /device:TPU:1, one launch (start us, length us, event | category | flops | bytes accessed | tf_op | source)
XLA Modules:
  0.0 383.9 jit_solution(6255276534862216508)
XLA Ops:
  7.2 0.0 copy-start
  7.2 0.0 all-gather.2.cloned.1.call-start
  7.2 0.7 all-gather.2.cloned.1.call-update
  7.9 0.0 all-reduce.5.cloned.1.call-start
  8.0 0.8 broadcast_compare_fusion
  8.8 0.1 broadcast_bitcast_fusion
  8.9 0.8 dynamic-slice_subtract_fusion
  9.6 0.1 iota_compare_fusion
  9.7 49.3 %all-gather.2.cloned.1.call-done = bf16[2,6144,256]{2,1,0:T(8,128)(2,1)} async-done(((bf16[2,384,256]{2,1,0:T(8,128)(2,1)}), bf16[2,6144,256]{2,1,0:T(8,128)(2,1)}) %all-gather.2.cloned.1.call-update) | async-done | bytes 6291472 | tf_op jit(solution)/shard_map/all_gather | solution.py:64
  59.0 1.0 constant_dynamic-slice_fusion
  60.0 0.1 broadcast_select_fusion
  60.1 0.8 fusion.1
  60.9 0.5 convolution_bitcast_fusion.1
  61.4 0.4 stack.9
  61.9 1.5 convolution_bitcast_fusion
  63.4 0.4 stack.10
  63.8 0.3 constant_dynamic-update-slice_fusion.1
  64.1 0.3 constant_dynamic-update-slice_fusion
  64.4 1.2 fusion
  65.6 1.0 copy.11
  66.6 1.0 copy.10
  67.6 0.0 copy-start.3
  67.6 0.2 broadcast_select_fusion.2
  67.8 0.8 copy-done.3
  68.6 1.7 convolution_bitcast_fusion.2
  70.3 0.0 all-reduce.5.cloned.1.call-update
  70.3 0.0 copy-start.5
  70.3 0.0 all-reduce.7.cloned.1.call-start
  70.4 161.8 %all-reduce.5.cloned.1.call-done = (f32[2,384,256]{2,1,0:T(8,128)}, f32[2,256,256]{1,2,0:T(8,128)}) async-done(((f32[2,384,256]{2,1,0:T(8,128)}, f32[2,256,256]{1,2,0:T(8,128)}), (f32[2,384,256]{2,1,0:T(8,128)}, f32[2,256,256]{1,2,0:T(8,128)})) %all-reduce.5.cloned.1.call-update) | async-done | bytes 1310736 | tf_op jit(solution)/shard_map/psum | solution.py:77
  232.2 1.0 broadcast_select_fusion.1
  233.2 0.0 all-reduce.7.cloned.1.call-update
  233.2 0.1 iota_compare_fusion.1
  233.3 0.1 broadcast_in_dim.93
  233.4 0.1 broadcast_in_dim.107
  233.5 0.2 copy.15
  233.7 0.6 copy-done.2
  234.3 0.4 copy.12
  234.7 1.7 broadcast_in_dim.104
  236.4 2.5 broadcast_in_dim.105
  238.9 1.3 select_negate_fusion
  240.2 3.0 copy.16
  243.2 126.0 %all-reduce.7.cloned.1.call-done = (f32[2,3,128,256]{3,2,1,0:T(8,128)}, f32[2,256,256]{1,2,0:T(8,128)}) async-done(((f32[2,3,128,256]{3,2,1,0:T(8,128)}, f32[2,256,256]{1,2,0:T(8,128)}), (f32[2,3,128,256]{3,2,1,0:T(8,128)}, f32[2,256,256]{1,2,0:T(8,128)})) %all-reduce.7.cloned.1.call-update) | async-done | bytes 1310736 | tf_op jit(solution)/shard_map/psum | solution.py:16
  369.3 1.2 add.50
  370.4 1.0 copy.17
  371.4 0.4 copy.13
  371.8 1.7 broadcast_in_dim.112
  373.5 2.5 broadcast_in_dim.113
  376.1 1.3 negate_bitcast_fusion
  (12 shorter events, 0.1 us)
Async XLA Ops:
  7.2 53.8 %copy-start = (bf16[768,768]{1,0:T(8,128)(2,1)S(1)}, bf16[768,768]{1,0:T(8,128)(2,1)}, u32[]{:S(2)}) copy-start(bf16[768,768]{1,0:T(8,128)(2,1)} %param.4) | copy-start | bytes 3538948
  7.2 51.8 %all-gather.2.cloned.1.call-start = ((), (), s32[]{:S(2)}) async-start(), calls=%async_computation | async-start | bytes 6684672 | tf_op jit(solution)/shard_map/all_gather | solution.py:64
  7.9 224.3 %all-reduce.5.cloned.1.call-start = ((), (), s32[]{:S(2)}) async-start(), calls=%async_computation.1 | async-start | bytes 2621440 | tf_op jit(solution)/shard_map/psum | solution.py:77
  67.6 1.0 copy-start.3
  68.6 1.7 copy-start.1
  70.3 163.2 %copy-start.5 = (f32[2,256,256]{2,1,0:T(8,128)S(1)}, f32[2,256,256]{2,1,0:T(8,128)}, u32[]{:S(2)}) copy-start(f32[2,256,256]{2,1,0:T(8,128)} %param.7) | copy-start | bytes 1572868
  70.3 298.9 %all-reduce.7.cloned.1.call-start = ((), (), s32[]{:S(2)}) async-start(), calls=%async_computation.2 | async-start | bytes 2621440 | tf_op jit(solution)/shard_map/psum | solution.py:16
  233.2 1.1 copy-start.2
  369.3 2.2 copy-start.4
Sparse Core Ops, SparseCore 0:
  9.8 49.1 all-gather.1
  70.4 161.7 all-reduce.4
  234.9 134.2 all-reduce.6
